TPU v7x, 32 devices: a whole 2x2x4 slice. The times are simulated.
32 devices in a mesh: rep: 4 (over x, core), shard: 8 (over z, y).
Axes of the slice: x: 2, y: 2, z: 4, core: 2. Of those that a mesh axis runs over, the one named last changes fastest.
Arguments:
- residual: float32 [4, 1024, 768], P('rep', 'shard'), may hold values from -6 to 6
- segment_ids: int32 [4, 1024], P('rep', 'shard'), may hold values from 0 to 7, never falling along the last dimension, each value on 1 to 256 neighbouring positions
- in_weight: bfloat16 [2, 768, 3352], P(None, 'shard'), may hold values from -0.21875 to 0.21875
- conv_weight: bfloat16 [2, 4, 1792], P(None, None, 'shard'), may hold values from -3 to 3
- conv_bias: bfloat16 [2, 1792], P(None, 'shard'), may hold values from -3 to 3
- a_log: float32 [2, 24], replicated, may hold values from -2 to 2.5
- dt_bias: float32 [2, 24], replicated, may hold values from -7 to -2
- d_skip: float32 [2, 24], replicated, may hold values from 0.5 to 1.5
- norm_gain: bfloat16 [2, 768], P(None, 'shard'), may hold values from 0.5 to 1.5
- gated_gain: bfloat16 [2, 1536], P(None, 'shard'), may hold values from 0.5 to 1.5
- out_weight: bfloat16 [2, 1536, 768], P(None, 'shard'), may hold values from -0.3125 to 0.3125
- out_cotangent: float32 [4, 1024, 768], P('rep', 'shard'), may hold values from -6 to 6
Outputs:
- output: float32 [4, 1024, 768], P('rep', 'shard')
- grad_input: float32 [4, 1024, 768], P('rep', 'shard')
- grad_in_weight: float32 [2, 768, 3352], P(None, 'shard')
- grad_conv_weight: float32 [2, 4, 1792], P(None, None, 'shard')
- grad_conv_bias: float32 [2, 1792], P(None, 'shard')
- grad_a_log: float32 [2, 24], replicated
- grad_dt_bias: float32 [2, 24], replicated
- grad_d_skip: float32 [2, 24], replicated
- grad_norm_gain: float32 [2, 768], P(None, 'shard')
- grad_gated_gain: float32 [2, 1536], P(None, 'shard')
- grad_out_weight: float32 [2, 1536, 768], P(None, 'shard')
Inputs may be any that keep to these rules, and one draw needn't show every extreme that they name: `segment_ids`: in each sequence the ids never fall; each document has 1 to 256 tokens and one has exactly 256.
All inputs are finite; a program needn't handle non-finite values.
Results may differ from a plain program's by a relative error of at most 0.011.
Values may be sent and summed in bfloat16 or wider, within the bound.
No kernel may reach another device: no remote copies, remote signals or barrier semaphores. Data moves between devices by JAX's collectives and lax.ppermute only.
A program may use at most 256 MiB of HBM per device.

v0:
```python
from functools import partial
import jax
import jax.numpy as jnp
from jax import lax
from jax.sharding import PartitionSpec as P

HEADS = 24
STATE = 128
HEADDIM = 64
CONV = 4
SPAN = 128
INNER = 1536
CONVDIM = 1792
EPS = 1e-05
HIGH = lax.Precision.HIGHEST


def passed_along(x, axis, by):
    count = lax.axis_size(axis)
    pairs = [(i, i + by) for i in range(count) if 0 <= i + by < count]
    return lax.ppermute(x, axis, pairs)


def carried_in(part, axis, combine, identity, reverse):
    count = lax.axis_size(axis)
    place = lax.axis_index(axis)
    ahead = count - 1 - place if reverse else place
    gathered = jax.tree.map(lambda a: lax.all_gather(a, axis), part)
    state = jax.tree.map(lambda a, e: jnp.zeros_like(a) + jnp.asarray(e, a.dtype), part, identity)

    def one(turn, state):
        source = count - 1 - turn if reverse else turn
        return combine(
            state, jax.tree.map(lambda a: lax.dynamic_index_in_dim(a, source, 0, False), gathered)
        )

    return lax.fori_loop(0, ahead, one, state)


def rms(values, gain):
    return values * lax.rsqrt(jnp.mean(values * values, axis=-1, keepdims=True) + EPS) * gain


def span_step(carry, pieces):
    state, last = carry
    xs, bs, cs, dts, das, segs = pieces
    width = segs.shape[0]
    cum = jnp.cumsum(das, axis=0)
    rows = lax.broadcasted_iota(jnp.int32, (width, width), 0)
    cols = lax.broadcasted_iota(jnp.int32, (width, width), 1)
    mask = ((rows >= cols) & (segs[:, None] == segs[None, :])).astype(jnp.float32)
    cum_t = cum.T
    diff = cum_t[:, :, None] - cum_t[:, None, :]
    lmat = jnp.exp(jnp.where(mask[None] > 0, diff, 0.0)) * mask[None]
    scores = jnp.dot(cs, bs.T, precision=HIGH)
    mixing = lmat * scores[None] * dts.T[:, None, :]
    inside = jnp.einsum("hij,jhp->ihp", mixing, xs, precision=HIGH)
    valid = (segs == last).astype(jnp.float32)
    carried = jnp.einsum("in,hnp->ihp", cs, state, precision=HIGH)
    carried = carried * (jnp.exp(cum) * valid[:, None])[:, :, None]
    tail = (segs == segs[-1]).astype(jnp.float32)
    decay = jnp.exp(cum[-1][None, :] - cum) * tail[:, None] * dts
    keep = jnp.exp(cum[-1]) * (segs[-1] == last).astype(jnp.float32)
    fresh = jnp.einsum("jh,jn,jhp->hnp", decay, bs, xs, precision=HIGH)
    return ((state * keep[:, None, None] + fresh, segs[-1]), inside + carried)


def front(xbc, rim, dt_raw, conv_w, conv_b, dtb, alog, keeps):
    length = xbc.shape[0]
    padded = jnp.concatenate([rim, xbc], 0)
    total = conv_b
    for k in range(CONV):
        total = total + conv_w[k] * padded[k : k + length] * keeps[k][:, None]
    conv_out = jax.nn.silu(total)
    xs = conv_out[:, :INNER].reshape(length, HEADS, HEADDIM)
    bs = conv_out[:, INNER : INNER + STATE]
    cs = conv_out[:, INNER + STATE :]
    dts = jax.nn.softplus(dt_raw + dtb)
    return (xs, bs, cs, dts, -dts * jnp.exp(alog))


def local_states(xs, bs, cs, dts, das, seg, seg_prev):
    length = seg.shape[0]
    count = length // SPAN
    pieces = (
        xs.reshape(count, SPAN, HEADS, HEADDIM),
        bs.reshape(count, SPAN, STATE),
        cs.reshape(count, SPAN, STATE),
        dts.reshape(count, SPAN, HEADS),
        das.reshape(count, SPAN, HEADS),
        seg.reshape(count, SPAN),
    )
    start = (jnp.zeros((HEADS, STATE, HEADDIM), jnp.float32), seg[0])
    (final, _), ys = lax.scan(span_step, start, pieces)
    passing = jnp.exp(jnp.sum(das, axis=0)) * (seg[-1] == seg_prev).astype(jnp.float32)
    return (ys.reshape(length, HEADS, HEADDIM), passing, final)


def finish(z_part, xs, cs, das, y_local, entering, dskip, ggain, seg, seg_prev):
    length = seg.shape[0]
    cum = jnp.cumsum(das, axis=0)
    valid = (seg == seg_prev).astype(jnp.float32)
    from_before = jnp.einsum("tn,hnp->thp", cs, entering, precision=HIGH)
    from_before = from_before * (jnp.exp(cum) * valid[:, None])[:, :, None]
    ys = y_local + from_before + dskip[None, :, None] * xs
    gated = ys.reshape(length, INNER) * jax.nn.silu(z_part)
    return rms(gated, ggain)


def combine(earlier, later):
    return (earlier[0] * later[0], later[0][:, None, None] * earlier[1] + later[1])


def gather_layer(
    in_weight, out_weight, conv_weight, conv_bias, norm_gain, gated_gain, layer, again
):
    if again:
        return (
            lax.all_gather(in_weight[layer], "shard", axis=0, tiled=True),
            lax.all_gather(out_weight[layer], "shard", axis=0, tiled=True),
            lax.all_gather(conv_weight[layer], "shard", axis=1, tiled=True),
            lax.all_gather(conv_bias[layer], "shard", axis=0, tiled=True),
            lax.all_gather(norm_gain[layer], "shard", axis=0, tiled=True),
            lax.all_gather(gated_gain[layer], "shard", axis=0, tiled=True),
        )
    return (
        lax.all_gather(in_weight[layer], "shard", axis=0, tiled=True),
        lax.all_gather(out_weight[layer], "shard", axis=0, tiled=True),
        lax.all_gather(conv_weight[layer], "shard", axis=1, tiled=True),
        lax.all_gather(conv_bias[layer], "shard", axis=0, tiled=True),
        lax.all_gather(norm_gain[layer], "shard", axis=0, tiled=True),
        lax.all_gather(gated_gain[layer], "shard", axis=0, tiled=True),
    )


def per_device(
    residual,
    segment_ids,
    in_weight,
    conv_weight,
    conv_bias,
    a_log,
    dt_bias,
    d_skip,
    norm_gain,
    gated_gain,
    out_weight,
    out_cotangent,
):
    u_now = residual[0]
    seg = segment_ids[0]
    length = seg.shape[0]
    layers = in_weight.shape[0]
    rim_ids = passed_along(seg[length - CONV + 1 :], "shard", 1)
    seg_ext = jnp.concatenate([rim_ids, seg])
    seg_prev = rim_ids[CONV - 2]
    keeps = jnp.stack([(seg_ext[k : k + length] == seg).astype(jnp.float32) for k in range(CONV)])
    identity = (jnp.ones((HEADS,), jnp.float32), jnp.zeros((HEADS, STATE, HEADDIM), jnp.float32))
    saved = []
    for layer in range(layers):
        weights = gather_layer(
            in_weight, out_weight, conv_weight, conv_bias, norm_gain, gated_gain, layer, False
        )
        w_in, w_out, conv_w, conv_b, n_gain, g_gain = weights
        normed, norm_pull = jax.vjp(rms, u_now, n_gain.astype(jnp.float32))
        hidden = normed.astype(jnp.bfloat16)
        proj = jnp.dot(hidden, w_in, preferred_element_type=jnp.float32)
        z_part = proj[:, :INNER]
        xbc = proj[:, INNER : INNER + CONVDIM]
        dt_raw = proj[:, INNER + CONVDIM :]
        rim = passed_along(xbc[length - CONV + 1 :], "shard", 1)
        feats, front_pull = jax.vjp(
            partial(front, keeps=keeps),
            xbc,
            rim,
            dt_raw,
            conv_w.astype(jnp.float32),
            conv_b.astype(jnp.float32),
            dt_bias[layer],
            a_log[layer],
        )
        xs, bs, cs, dts, das = feats
        (y_local, passing, final), local_pull = jax.vjp(
            partial(local_states, seg=seg, seg_prev=seg_prev), xs, bs, cs, dts, das
        )
        entering = carried_in((passing, final), "shard", combine, identity, False)[1]
        yn, finish_pull = jax.vjp(
            partial(finish, seg=seg, seg_prev=seg_prev),
            z_part,
            xs,
            cs,
            das,
            y_local,
            entering,
            d_skip[layer],
            g_gain.astype(jnp.float32),
        )
        yn_b = yn.astype(jnp.bfloat16)
        u_now = u_now + jnp.dot(yn_b, w_out, preferred_element_type=jnp.float32)
        kept = None
        saved.append(
            (hidden, norm_pull, front_pull, local_pull, finish_pull, passing, entering, yn_b, kept)
        )
    grad = out_cotangent[0]
    owned = [None] * layers
    heads = [None] * layers
    for layer in reversed(range(layers)):
        hidden, norm_pull, front_pull, local_pull, finish_pull, passing, entering, yn_b, kept = (
            saved[layer]
        )
        weights = gather_layer(
            in_weight, out_weight, conv_weight, conv_bias, norm_gain, gated_gain, layer, True
        )
        w_in, w_out = (weights[0], weights[1])
        grad_b = grad.astype(jnp.bfloat16)
        g_out = jnp.dot(yn_b.T, grad_b, preferred_element_type=jnp.float32)
        d_yn = jnp.dot(grad_b, w_out.T, preferred_element_type=jnp.float32)
        d_z, d_xs1, d_cs1, d_das1, d_local, d_enter, g_dsk, g_gg = finish_pull(d_yn)
        later = carried_in((passing, d_enter), "shard", combine, identity, True)[1]
        d_passing = jnp.sum(later * entering, axis=(1, 2))
        d_xs2, d_bs, d_cs2, d_dts, d_das2 = local_pull((d_local, d_passing, later))
        d_xbc, d_rim, d_dtr, g_cw, g_cb, g_dtb, g_alog = front_pull(
            (d_xs1 + d_xs2, d_bs, d_cs1 + d_cs2, d_dts, d_das1 + d_das2)
        )
        back_rim = passed_along(d_rim, "shard", -1)
        d_xbc = d_xbc.at[length - CONV + 1 :].add(back_rim)
        d_proj = jnp.concatenate([d_z, d_xbc, d_dtr], 1).astype(jnp.bfloat16)
        g_in = jnp.dot(hidden.T, d_proj, preferred_element_type=jnp.float32)
        d_h = jnp.dot(d_proj, w_in.T, preferred_element_type=jnp.float32)
        d_u, g_ng = norm_pull(d_h)
        grad = grad + d_u
        shares = (
            lax.psum_scatter(g_in, "shard", scatter_dimension=0, tiled=True),
            lax.psum_scatter(g_out, "shard", scatter_dimension=0, tiled=True),
            lax.psum_scatter(g_cw, "shard", scatter_dimension=1, tiled=True),
            lax.psum_scatter(g_cb, "shard", scatter_dimension=0, tiled=True),
            lax.psum_scatter(g_ng, "shard", scatter_dimension=0, tiled=True),
            lax.psum_scatter(g_gg, "shard", scatter_dimension=0, tiled=True),
        )
        shares = lax.psum((shares[0], shares[1], shares[2], shares[3], shares[4], shares[5]), "rep")
        owned[layer] = shares
        heads[layer] = jnp.stack([g_alog, g_dtb, g_dsk])
    grads_in = jnp.stack([owned[k][0] for k in range(layers)])
    grads_out = jnp.stack([owned[k][1] for k in range(layers)])
    grads_cw = jnp.stack([owned[k][2] for k in range(layers)])
    grads_cb = jnp.stack([owned[k][3] for k in range(layers)])
    grads_ng = jnp.stack([owned[k][4] for k in range(layers)])
    grads_gg = jnp.stack([owned[k][5] for k in range(layers)])
    head_sums = lax.psum(jnp.stack(heads), ("rep", "shard"))
    return (
        u_now[None],
        grad[None],
        grads_in,
        grads_cw,
        grads_cb,
        head_sums[:, 0],
        head_sums[:, 1],
        head_sums[:, 2],
        grads_ng,
        grads_gg,
        grads_out,
    )


def solution(mesh):
    return jax.shard_map(
        per_device,
        mesh=mesh,
        in_specs=(
            P("rep", "shard", None),
            P("rep", "shard"),
            P(None, "shard", None),
            P(None, None, "shard"),
            P(None, "shard"),
            P(),
            P(),
            P(),
            P(None, "shard"),
            P(None, "shard"),
            P(None, "shard", None),
            P("rep", "shard", None),
        ),
        out_specs=(
            P("rep", "shard", None),
            P("rep", "shard", None),
            P(None, "shard", None),
            P(None, None, "shard"),
            P(None, "shard"),
            P(),
            P(),
            P(),
            P(None, "shard"),
            P(None, "shard"),
            P(None, "shard", None),
        ),
        check_vma=False,
    )
```

profile of v0, /device:TPU:0, one launch (start us, length us, event | category | flops | bytes accessed | tf_op | source)
XLA Modules:
  0.0 1677.2 jit_solution(14095411536137109909)
XLA Ops:
  9.9 4.9 collective-permute-start.1
  18.8 37.3 %all-reduce.43 = (bf16[768]{0:T(1024)(128)(2,1)S(1)}, bf16[1792]{0:T(1024)(128)(2,1)S(1)}, bf16[1536]{0:T(1024)(128)(2,1)S(1)}, bf16[768]{0:T(1024)(128)(2,1)S(1...) all-reduce(bf16[768]{0:T(1024)(128)(2,1)S(1)} %dynamic-update-slice, ...), channel_id=4, replica_groups=mesh['rep'=4,'shard'=8] {'shard'}, use_global_device_ids=true, to_apply=%add.27 | all-reduce | flops 8192 | bytes 32768
  56.3 36.0 %all-gather.1 = bf16[1,4,1792]{1,0,2:T(2,128)(2,1)S(1)} all-gather(bf16[1,4,224]{1,0,2:T(2,128)(2,1)S(1)} %copy.431), channel_id=3, replica_groups=mesh['rep'=4,'shard'=8] {'shard'}, dimensions={2}, use_global_device_ids=true | all-gather | bytes 16128 | tf_op jit(solution)/shard_map/all_gather | solution.py:129
  96.0 37.5 %slice_reduce_fusion.7 = (f32[1792]{0:T(1024)S(1)}, f32[1792]{0:T(1024)S(1)}, f32[1792]{0:T(1024)S(1)}, f32[1792]{0:T(1024)S(1)}) fusion(f32[1,4,1792]{1,0,2:T(1,128)S(1)} %convert_element_type.131), kind=kLoop, calls=%fused_computation.128 | loop fusion | bytes 57344 | tf_op jit(solution)/shard_map/jvp()/slice | solution.py:73
  146.3 5.4 fusion.102
  158.1 36.8 %all-gather.9 = bf16[1,4,1792]{1,0,2:T(2,128)(2,1)S(1)} all-gather(bf16[1,4,224]{1,0,2:T(2,128)(2,1)S(1)} %copy.432), channel_id=11, replica_groups=mesh['rep'=4,'shard'=8] {'shard'}, dimensions={2}, use_global_device_ids=true | all-gather | bytes 16128 | tf_op jit(solution)/shard_map/all_gather | solution.py:129
  197.8 37.7 %slice_reduce_fusion.3 = (f32[1792]{0:T(1024)}, f32[1792]{0:T(1024)}, f32[1792]{0:T(1024)}, f32[1792]{0:T(1024)}) fusion(f32[1,4,1792]{1,0,2:T(1,128)S(1)} %convert_element_type.135), kind=kLoop, calls=%fused_computation.123 | loop fusion | bytes 57344 | tf_op jit(solution)/shard_map/jvp()/slice | solution.py:73
  236.9 19.7 %all-reduce.28 = f32[192]{0:T(256)S(1)} all-reduce(f32[192]{0:T(256)S(1)} %multiply_dynamic-update-slice_fusion.1), channel_id=6, replica_groups=mesh['rep'=4,'shard'=8] {'shard'}, use_global_device_ids=true, to_apply=%add.28 | all-reduce | flops 192 | bytes 1536
  269.5 43.2 %all-gather.31.cloned.1.call-done = bf16[1,1536,768]{2,1,0:T(8,128)(2,1)} async-done(((bf16[1,192,768]{2,1,0:T(8,128)(2,1)}), bf16[1,1536,768]{2,1,0:T(8,128)(2,1)}) %all-gather.31.cloned.1.call-update) | async-done | bytes 2359312 | tf_op jit(solution)/shard_map/all_gather | solution.py:128
  315.9 84.1 %all-gather.33.cloned.1.call-done = bf16[1,768,3352]{2,1,0:T(8,128)(2,1)} async-done(((bf16[1,96,3352]{2,1,0:T(8,128)(2,1)}), bf16[1,768,3352]{2,1,0:T(8,128)(2,1)}) %all-gather.33.cloned.1.call-update) | async-done | bytes 5148688 | tf_op jit(solution)/shard_map/all_gather | solution.py:127
  417.6 5.4 fusion.101
  426.5 19.1 %all-reduce.32 = f32[192]{0:T(256)S(1)} all-reduce(f32[192]{0:T(256)S(1)} %multiply_dynamic-update-slice_fusion), channel_id=14, replica_groups=mesh['rep'=4,'shard'=8] {'shard'}, use_global_device_ids=true, to_apply=%add.32 | all-reduce | flops 192 | bytes 1536
  447.8 75.4 %all-gather.35.cloned.1.call-done = f32[192,128,64]{1,2,0:T(8,128)} async-done(((f32[24,128,64]{1,2,0:T(8,128)}), f32[192,128,64]{1,2,0:T(8,128)}) %all-gather.35.cloned.1.call-update) | async-done | bytes 6291472 | tf_op jit(solution)/shard_map/all_gather | solution.py:28
  535.1 40.7 %all-gather.37.cloned.1.call-done = bf16[1,1536,768]{2,1,0:T(8,128)(2,1)} async-done(((bf16[1,192,768]{2,1,0:T(8,128)(2,1)}), bf16[1,1536,768]{2,1,0:T(8,128)(2,1)}) %all-gather.37.cloned.1.call-update) | async-done | bytes 2359312 | tf_op jit(solution)/shard_map/all_gather | solution.py:128
  594.6 91.4 %all-gather.39.cloned.1.call-done = f32[192,128,64]{1,2,0:T(8,128)} async-done(((f32[24,128,64]{1,2,0:T(8,128)}), f32[192,128,64]{1,2,0:T(8,128)}) %all-gather.39.cloned.1.call-update) | async-done | bytes 6291472 | tf_op jit(solution)/shard_map/all_gather | solution.py:28
  687.4 50.6 %while.36 = (s32[]{:T(128)}, f32[24,128,64]{2,1,0:T(8,128)}, s32[]{:T(128)}, f32[8,24]{1,0:T(8,128)}, f32[8,24,128,64]{2,3,1,0:T(8,128)}, /*index=5*/s32[]{:T(128)}, s32[]{:T(128)}, s32[]{:T(128)}, s32[]{:T(128)}) while((s32[]{:T(128)}, f32[24,128,64]{2,1,0:T(8,128)}, s32[]{:T(128)}, f32[8,24]{1,0:T(8,128)}, f32[8,24,128,64]{2,3,1,0:T(8,128)}, ...), condition=%wide.region_15.17_spmd, body=%wide.region_14.16_spmd.sunk | while | flops 393222 | bytes 5505467 | solution.py:37
  773.8 6.0 scatter-add.6
  779.9 5.1 multiply_reduce_fusion.30
  808.5 6.7 fusion.173
  830.1 59.3 %all-gather.41.cloned.1.call-done = f32[192,128,64]{1,2,0:T(8,128)} async-done(((f32[24,128,64]{1,2,0:T(8,128)}), f32[192,128,64]{1,2,0:T(8,128)}) %all-gather.41.cloned.1.call-update) | async-done | bytes 6291472 | tf_op jit(solution)/shard_map/all_gather | solution.py:28
  890.7 50.3 %while.37 = (s32[]{:T(128)}, f32[24,128,64]{2,1,0:T(8,128)}, s32[]{:T(128)}, f32[8,24]{1,0:T(8,128)}, f32[8,24,128,64]{2,3,1,0:T(8,128)}, /*index=5*/s32[]{:T(128)}, s32[]{:T(128)}, s32[]{:T(128)}, s32[]{:T(128)}) while((s32[]{:T(128)}, f32[24,128,64]{2,1,0:T(8,128)}, s32[]{:T(128)}, f32[8,24]{1,0:T(8,128)}, f32[8,24,128,64]{2,3,1,0:T(8,128)}, ...), condition=%wide.region_30.32_spmd, body=%wide.region_29.31_spmd.sunk | while | flops 393222 | bytes 5505467 | solution.py:37
  941.0 5.3 multiply_reduce_fusion.16
  989.4 6.0 scatter-add.9
  995.4 6.7 fusion.172
  1010.4 42.3 %reduce-scatter.17.cloned.1.call-done = f32[192,768]{1,0:T(8,128)} async-done(((f32[1536,768]{1,0:T(8,128)}), f32[192,768]{1,0:T(8,128)}) %reduce-scatter.17.cloned.1.call-update) | async-done | bytes 589840 | tf_op jit(solution)/shard_map/reduce_scatter | solution.py:234
  1052.7 99.0 %reduce-scatter.15.cloned.1.call-done = f32[192,768]{1,0:T(8,128)} async-done(((f32[1536,768]{1,0:T(8,128)}), f32[192,768]{1,0:T(8,128)}) %reduce-scatter.15.cloned.1.call-update) | async-done | bytes 589840 | tf_op jit(solution)/shard_map/reduce_scatter | solution.py:234
  1151.7 183.2 %reduce-scatter.13.cloned.1.call-done = f32[96,3352]{1,0:T(8,128)} async-done(((f32[768,3352]{1,0:T(8,128)}), f32[96,3352]{1,0:T(8,128)}) %reduce-scatter.13.cloned.1.call-update) | async-done | bytes 1287184 | tf_op jit(solution)/shard_map/reduce_scatter | solution.py:233
  1334.9 182.8 %reduce-scatter.11.cloned.1.call-done = f32[96,3352]{1,0:T(8,128)} async-done(((f32[768,3352]{1,0:T(8,128)}), f32[96,3352]{1,0:T(8,128)}) %reduce-scatter.11.cloned.1.call-update) | async-done | bytes 1287184 | tf_op jit(solution)/shard_map/reduce_scatter | solution.py:233
  1517.8 39.6 %psum.97 = f32[2,3,24]{2,1,0:T(4,128)S(1)} all-reduce(f32[2,3,24]{2,1,0:T(4,128)S(1)} %pad_maximum_fusion.11), channel_id=1, replica_groups=mesh['rep'=4,'shard'=8] {'rep','shard'}, use_global_device_ids=true, to_apply=%region_72.74 | all-reduce | flops 144 | bytes 1152 | tf_op jit(solution)/shard_map/psum | solution.py:249
  1562.4 37.4 %all-reduce.40 = (f32[1792]{0:T(1024)S(1)}, f32[1792]{0:T(1024)S(1)}, f32[768]{0:T(1024)S(1)}, f32[768]{0:T(1024)S(1)}, f32[1536]{0:T(1024)S(1)}, /*index=5*/f32[1536]{0:T(1024)S(1)}) all-reduce(f32[1792]{0:T(1024)S(1)} %copy-done.120, f32[1792]{0:T(1024)S(1)} %get-tuple-element.833, ...), channel_id=25, replica_groups=mesh['rep'=4,'shard'=8] {'shard'}, use_global_device_ids=true, to_apply=%region_62.64.clone | all-reduce | flops 8192 | bytes 65536
  1602.1 11.7 all-reduce.41
  1616.1 49.8 %all-reduce.46.cloned.1.call-done = (f32[1,96,3352]{2,1,0:T(8,128)}, f32[1,96,3352]{2,1,0:T(8,128)}, f32[1,192,768]{2,1,0:T(8,128)}, f32[1,192,768]{2,1,0:T(8,128)}) async-done(((f32[1,96,3352]{2,1,0:T(8,128)}, f32[1,96,3352]{2,1,0:T(8,128)}, f32[1,192,768]{2,1,0:T(8,128)}, f32[1,192,768]{2,1,0:T(8,128)}), (f32[1,96,3352]{2,1,0:T(8,128)}, f32[1,96,3352]{2,1,0:T(8,128)}, f32[1,192,768]{2,1,0:T(8,128)}, ...) | async-done | bytes 3754000 | tf_op jit(solution)/shard_map/psum | solution.py:240
  (745 shorter events, 337.1 us)
Async XLA Ops:
  7.2 48.9 %copy-start.193 = (bf16[2,4,224]{2,1,0:T(4,128)(2,1)S(1)}, bf16[2,4,224]{2,1,0:T(4,128)(2,1)}, u32[]{:S(2)}) copy-start(bf16[2,4,224]{2,1,0:T(4,128)(2,1)} %param.28) | copy-start | bytes 10756
  7.2 129.0 %all-gather.27.cloned.1.call-start = ((), (), s32[]{:S(2)}) async-start(), calls=%async_computation.10 | async-start | bytes 5971968 | tf_op jit(solution)/shard_map/all_gather | solution.py:127
  9.8 250.9 %all-gather.29.cloned.1.call-start = ((), (), s32[]{:S(2)}) async-start(), calls=%async_computation.11 | async-start | bytes 7077888 | tf_op jit(solution)/shard_map/all_gather | solution.py:28
  9.9 123.7 %collective-permute-start.1 = (s32[3]{0:T(128)S(1)}, s32[3]{0:T(128)S(1)}, u32[]{:S(2)}, u32[]{:S(2)}) collective-permute-start(s32[3]{0:T(128)S(1)} %slice_bitcast_fusion.5), channel_id=1, source_target_pairs={{0,1},{1,2},{2,3},{3,4},{4,5},{5,6},{6,7},{8,9},{9,10},{10,11},{11... | collective-permute-start | bytes 44 | tf_op jit(solution)/shard_map/ppermute | solution.py:21
  14.8 80.4 %copy-start.30 = (f32[1,128,768]{2,1,0:T(8,128)S(1)}, f32[1,128,768]{2,1,0:T(8,128)}, u32[]{:S(2)}) copy-start(f32[1,128,768]{2,1,0:T(8,128)} %param.25) | copy-start | bytes 1179652
  96.0 46.9 %copy-start.182 = (f32[24]{0:T(128)}, f32[24]{0:T(128)S(1)}, u32[]{:S(2)}) copy-start(f32[24]{0:T(128)S(1)} %get-tuple-element.1008) | copy-start | bytes 292
  96.0 48.3 %copy-start.138 = (f32[24]{0:T(128)}, f32[24]{0:T(128)S(1)}, u32[]{:S(2)}) copy-start(f32[24]{0:T(128)S(1)} %get-tuple-element.984) | copy-start | bytes 292
  141.6 3.4 collective-permute-start
  143.7 93.1 %copy-start.185 = (f32[24]{0:T(128)}, f32[24]{0:T(128)S(1)}, u32[]{:S(2)}) copy-start(f32[24]{0:T(128)S(1)} %get-tuple-element.939) | copy-start | bytes 292
  151.7 107.2 %copy-start.25 = (f32[128,1792]{0,1:T(8,128)}, f32[128,1792]{0,1:T(8,128)S(1)}, u32[]{:S(2)}) copy-start(f32[128,1792]{0,1:T(8,128)S(1)} %get-tuple-element.941) | copy-start | bytes 2752516
  154.5 158.2 %all-gather.31.cloned.1.call-start = ((), (), s32[]{:S(2)}) async-start(), calls=%async_computation.12 | async-start | bytes 2654208 | tf_op jit(solution)/shard_map/all_gather | solution.py:128
  155.4 244.6 %all-gather.33.cloned.1.call-start = ((), (), s32[]{:S(2)}) async-start(), calls=%async_computation.13 | async-start | bytes 5971968 | tf_op jit(solution)/shard_map/all_gather | solution.py:127
  156.0 367.2 %all-gather.35.cloned.1.call-start = ((), (), s32[]{:S(2)}) async-start(), calls=%async_computation.14 | async-start | bytes 7077888 | tf_op jit(solution)/shard_map/all_gather | solution.py:28
  315.9 84.1 %copy-start.211 = (f32[128]{0:T(128)}, f32[128]{0:T(128)S(1)}, u32[]{:S(2)}) copy-start(f32[128]{0:T(128)S(1)} %get-tuple-element.998) | copy-start | bytes 1540
  315.9 88.9 %copy-start.179 = (f32[128]{0:T(128)}, f32[128]{0:T(128)S(1)}, u32[]{:S(2)}) copy-start(f32[128]{0:T(128)S(1)} %fusion.221) | copy-start | bytes 1540
  408.4 7.1 collective-permute-start.2
  425.7 150.1 %all-gather.37.cloned.1.call-start = ((), (), s32[]{:S(2)}) async-start(), calls=%async_computation.15 | async-start | bytes 2654208 | tf_op jit(solution)/shard_map/all_gather | solution.py:128
  426.3 259.7 %all-gather.39.cloned.1.call-start = ((), (), s32[]{:S(2)}) async-start(), calls=%async_computation.16 | async-start | bytes 7077888 | tf_op jit(solution)/shard_map/all_gather | solution.py:28
  426.4 152.8 %copy-start.73 = (f32[1536]{0:T(1024)}, f32[1536]{0:T(1024)S(1)}, u32[]{:S(2)}) copy-start(f32[1536]{0:T(1024)S(1)} %convert_element_type.143) | copy-start | bytes 18436
  445.7 143.3 %copy-start.164 = (f32[24,128]{1,0:T(8,128)}, f32[24,128]{1,0:T(8,128)S(1)}, u32[]{:S(2)}) copy-start(f32[24,128]{1,0:T(8,128)S(1)} %copy.318) | copy-start | bytes 36868
  446.1 143.0 %copy-start.102 = (f32[128,128]{1,0:T(8,128)}, f32[128,128]{1,0:T(8,128)S(1)}, u32[]{:S(2)}) copy-start(f32[128,128]{1,0:T(8,128)S(1)} %fusion.189) | copy-start | bytes 196612
  584.1 305.3 %all-gather.41.cloned.1.call-start = ((), (), s32[]{:S(2)}) async-start(), calls=%async_computation.17 | async-start | bytes 7077888 | tf_op jit(solution)/shard_map/all_gather | solution.py:28
  765.6 5.8 collective-permute-start.3
  792.6 215.3 %reduce-scatter.21.cloned.1.call-start = ((), (), s32[]{:S(2)}) async-start(), calls=%async_computation.19 | async-start | bytes 1032192
  798.2 254.5 %reduce-scatter.17.cloned.1.call-start = ((), (), s32[]{:S(2)}) async-start(), calls=%async_computation.9 | async-start | bytes 5308416 | tf_op jit(solution)/shard_map/reduce_scatter | solution.py:234
  802.4 349.2 %reduce-scatter.15.cloned.1.call-start = ((), (), s32[]{:S(2)}) async-start(), calls=%async_computation.8 | async-start | bytes 5308416 | tf_op jit(solution)/shard_map/reduce_scatter | solution.py:234
  807.6 527.4 %reduce-scatter.13.cloned.1.call-start = ((), (), s32[]{:S(2)}) async-start(), calls=%async_computation.7 | async-start | bytes 11943936 | tf_op jit(solution)/shard_map/reduce_scatter | solution.py:233
  815.3 702.4 %reduce-scatter.11.cloned.1.call-start = ((), (), s32[]{:S(2)}) async-start(), calls=%async_computation.6 | async-start | bytes 11943936 | tf_op jit(solution)/shard_map/reduce_scatter | solution.py:233
  828.3 62.4 %copy-start.71 = (f32[128,128]{1,0:T(8,128)}, f32[128,128]{1,0:T(8,128)S(1)}, u32[]{:S(2)}) copy-start(f32[128,128]{1,0:T(8,128)S(1)} %get-tuple-element.823) | copy-start | bytes 196612
  979.8 6.2 collective-permute-start.4
  1002.2 599.0 %reduce-scatter.19.cloned.1.call-start = ((), (), s32[]{:S(2)}) async-start(), calls=%async_computation.18 | async-start | bytes 1032192
  1010.3 655.6 %all-reduce.46.cloned.1.call-start = ((), (), s32[]{:S(2)}) async-start(), calls=%async_computation.20 | async-start | bytes 7667712 | tf_op jit(solution)/shard_map/psum | solution.py:240
  (202 other events, 1522.9 us)
Sparse Core Ops, SparseCore 0:
  10.8 104.5 all-gather.26
  154.6 105.1 all-gather.28
  262.6 50.0 all-gather.30
  314.7 85.2 all-gather.32
  425.8 97.3 all-gather.34
  525.8 49.9 all-gather.36
  584.2 101.7 all-gather.38
  792.7 96.5 all-gather.40
  892.7 62.0 reduce-scatter.20
  958.2 94.4 reduce-scatter.16
  1056.3 95.2 reduce-scatter.14
  1155.1 179.7 reduce-scatter.12
  1338.5 179.1 reduce-scatter.10
  1521.5 62.8 reduce-scatter.18
  1586.9 78.9 all-reduce.45
where the time goes:
time: 1680 us
  waiting for transfers between devices  956 us (57%)
  blocking collectives  238 us (14%)
  local copies, waits for them, and re-layouts  216 us (13%)
  other arithmetic  118 us (7%)
  matrix products  112 us (7%)
  between operations  24.3 us (1%)
    reduce_scatter x2, waiting for transfers between devices, per_device(): lax.psum_scatter(g_in, 'shard', scatter_dimension=0, tiled=True)  366 us
    all_gather x4, waiting for transfers between devices, carried_in(): gathered = jax.tree.map(lambda a: lax.all_gather(a, axis), part)  226 us
    reduce_scatter x2, waiting for transfers between devices, per_device(): lax.psum_scatter(g_out, 'shard', scatter_dimension=0, tiled=True)  141 us
    unnamed x4, blocking collectives  114 us
    all_gather x2, waiting for transfers between devices, gather_layer(): lax.all_gather(in_weight[layer], 'shard', axis=0, tiled=True)  84.1 us
    all_gather x2, waiting for transfers between devices, gather_layer(): lax.all_gather(out_weight[layer], 'shard', axis=0, tiled=True)  83.9 us
    slice x2, local copies, waits for them, and re-layouts, front(): total = total + conv_w[k] * padded[k:k + length] * keeps[k][:, None]  75.2 us
    all_gather x2, blocking collectives, gather_layer(): lax.all_gather(conv_weight[layer], 'shard', axis=1, tiled=True)  72.8 us
  transfers between devices with their start and end apart: 20, of which 13 were waited for; matrix products, arithmetic and copies ran while one was open for 17% of the time, Pallas kernels for 0%

commit v1 on v0

--- a/solution.py
+++ b/solution.py
@@ -13,6 +13,24 @@
 CONVDIM = 1792
 EPS = 1e-05
 HIGH = lax.Precision.HIGHEST
+
+
+def gather_around(array, axis, dim):
+    ways, here, step = (lax.axis_size(axis), lax.axis_index(axis), array.shape[dim])
+    dims = [n * ways if d == dim else n for d, n in enumerate(array.shape)]
+    full = lax.dynamic_update_slice_in_dim(
+        jnp.zeros(dims, array.dtype), array, here * step, axis=dim
+    )
+    going_up = going_down = array
+    for far in range(1, ways // 2 + 1):
+        going_up = lax.ppermute(going_up, axis, [(d, (d + 1) % ways) for d in range(ways)])
+        full = lax.dynamic_update_slice_in_dim(full, going_up, (here - far) % ways * step, axis=dim)
+        if 2 * far < ways:
+            going_down = lax.ppermute(going_down, axis, [(d, (d - 1) % ways) for d in range(ways)])
+            full = lax.dynamic_update_slice_in_dim(
+                full, going_down, (here + far) % ways * step, axis=dim
+            )
+    return full
 
 
 def passed_along(x, axis, by):
@@ -124,7 +142,7 @@
             lax.all_gather(gated_gain[layer], "shard", axis=0, tiled=True),
         )
     return (
-        lax.all_gather(in_weight[layer], "shard", axis=0, tiled=True),
+        gather_around(in_weight[layer], "shard", 0),
         lax.all_gather(out_weight[layer], "shard", axis=0, tiled=True),
         lax.all_gather(conv_weight[layer], "shard", axis=1, tiled=True),
         lax.all_gather(conv_bias[layer], "shard", axis=0, tiled=True),

time: 1680 us -> 1860 us (1.11)
  blocking collectives: 238 us -> 294 us
  waiting for transfers between devices: 956 us -> 1010 us
  starting transfers between devices: 12.8 us -> 63.2 us
  local copies, waits for them, and re-layouts: 216 us -> 235 us
    ppermute x0 -> x14, waiting for transfers between devices: none -> 83.2 us  [the longest x8 83.2 us: gather_around(): lax.ppermute(going_up, axis, [(d, (d + 1) % ways) for d in range(ways)])]
    ppermute x0 -> x14, starting transfers between devices: none -> 49.7 us  [the longest x6 34.4 us: gather_around(): lax.ppermute(going_down, axis, [(d, (d - 1) % ways) for d in range(ways)])]
    all_gather x2, waiting for transfers between devices: 83.9 us -> 40.7 us  [gather_layer(): lax.all_gather(out_weight[layer], 'shard', axis=0, tiled=True)]
    unnamed x4, blocking collectives: 114 us -> 157 us
    all_gather x2, waiting for transfers between devices: 84.1 us -> 46.2 us  [gather_layer(): lax.all_gather(in_weight[layer], 'shard', axis=0, tiled=True)]
    unnamed x17, waiting for transfers between devices: 1.28 us -> 26.9 us
  transfers between devices with their start and end apart: 20 -> 34, of which waited for: 13 -> 18; matrix products, arithmetic and copies ran while one was open for 17% -> 21% of each run, Pallas kernels for 0% -> 0%
where the time goes in v1:
time: 1860 us; the launch traced here: 1850 us
  waiting for transfers between devices  1010 us (54%)
  blocking collectives  294 us (16%)
  local copies, waits for them, and re-layouts  235 us (13%)
  other arithmetic  117 us (6%)
  matrix products  111 us (6%)
  starting transfers between devices  63.2 us (3%)
  between operations  24.3 us (1%)
    reduce_scatter x2, waiting for transfers between devices, per_device(): lax.psum_scatter(g_in, 'shard', scatter_dimension=0, tiled=True)  366 us
    all_gather x4, waiting for transfers between devices, carried_in(): gathered = jax.tree.map(lambda a: lax.all_gather(a, axis), part)  227 us
    unnamed x4, blocking collectives  157 us
    reduce_scatter x2, waiting for transfers between devices, per_device(): lax.psum_scatter(g_out, 'shard', scatter_dimension=0, tiled=True)  152 us
    all_gather x2, blocking collectives, gather_layer(): lax.all_gather(conv_weight[layer], 'shard', axis=1, tiled=True)  84.9 us
    ppermute x8, waiting for transfers between devices, gather_around(): lax.ppermute(going_up, axis, [(d, (d + 1) % ways) for d in range(ways)])  83.2 us
    slice x2, local copies, waits for them, and re-layouts, front(): total = total + conv_w[k] * padded[k:k + length] * keeps[k][:, None]  74.9 us
    psum x1, waiting for transfers between devices, per_device(): lax.psum((shares[0], shares[1], shares[2], shares[3], shares[4], shares[5...  67.1 us
  transfers between devices with their start and end apart: 34, of which 18 were waited for; matrix products, arithmetic and copies ran while one was open for 21% of the time, Pallas kernels for 0%

profile of v1, /device:TPU:0, one launch (start us, length us, event | category | flops | bytes accessed | tf_op | source)
XLA Modules:
  0.0 1854.9 jit_solution(3966138821309934395)
XLA Ops:
  21.6 51.6 %all-reduce.43 = (bf16[768]{0:T(1024)(128)(2,1)S(1)}, bf16[1792]{0:T(1024)(128)(2,1)S(1)}, bf16[1536]{0:T(1024)(128)(2,1)}, bf16[768]{0:T(1024)(128)(2,1)}, bf16...) all-reduce(bf16[768]{0:T(1024)(128)(2,1)S(1)} %dynamic-update-slice.7, ...), channel_id=4, replica_groups=mesh['rep'=4,'shard'=8] {'shard'}, use_global_device_ids=true, to_apply=%add.27 | all-reduce | flops 8192 | bytes 32768
  74.6 32.0 %all-gather.1 = bf16[1,4,1792]{1,0,2:T(2,128)(2,1)S(1)} all-gather(bf16[1,4,224]{1,0,2:T(2,128)(2,1)S(1)} %copy.431), channel_id=3, replica_groups=mesh['rep'=4,'shard'=8] {'shard'}, dimensions={2}, use_global_device_ids=true | all-gather | bytes 16128 | tf_op jit(solution)/shard_map/all_gather | solution.py:147
  107.6 37.1 %slice_reduce_fusion.7 = (f32[1792]{0:T(1024)S(1)}, f32[1792]{0:T(1024)S(1)}, f32[1792]{0:T(1024)S(1)}, f32[1792]{0:T(1024)S(1)}) fusion(f32[1,4,1792]{1,0,2:T(1,128)S(1)} %convert_element_type.131), kind=kLoop, calls=%fused_computation.124 | loop fusion | bytes 57344 | tf_op jit(solution)/shard_map/jvp()/slice | solution.py:91
  160.3 21.3 %collective-permute-done.2 = bf16[96,3352]{1,0:T(8,128)(2,1)S(1)} collective-permute-done((bf16[96,3352]{1,0:T(8,128)(2,1)S(1)}, bf16[96,3352]{1,0:T(8,128)(2,1)S(1)}, u32[]{:S(2)}, u32[]{:S(2)}) %collective-permute-start.2) | collective-permute-done | bytes 643616 | tf_op jit(solution)/shard_map/ppermute | solution.py:26
  184.0 16.8 collective-permute-start.5
  210.1 9.1 collective-permute-done.6
  253.3 52.9 %all-gather.8 = bf16[1,4,1792]{1,0,2:T(2,128)(2,1)S(1)} all-gather(bf16[1,4,224]{1,0,2:T(2,128)(2,1)S(1)} %copy.432), channel_id=10, replica_groups=mesh['rep'=4,'shard'=8] {'shard'}, dimensions={2}, use_global_device_ids=true | all-gather | bytes 16128 | tf_op jit(solution)/shard_map/all_gather | solution.py:147
  307.2 37.7 %slice_reduce_fusion.3 = (f32[1792]{0:T(1024)}, f32[1792]{0:T(1024)}, f32[1792]{0:T(1024)}, f32[1792]{0:T(1024)}) fusion(f32[1,4,1792]{1,0,2:T(1,128)S(1)} %convert_element_type.135), kind=kLoop, calls=%fused_computation.119 | loop fusion | bytes 57344 | tf_op jit(solution)/shard_map/jvp()/slice | solution.py:91
  354.5 20.9 %collective-permute-done.11 = bf16[96,3352]{1,0:T(8,128)(2,1)S(1)} collective-permute-done((bf16[96,3352]{1,0:T(8,128)(2,1)}, bf16[96,3352]{1,0:T(8,128)(2,1)S(1)}, u32[]{:S(2)}, u32[]{:S(2)}) %collective-permute-start.11) | collective-permute-done | bytes 643616 | tf_op jit(solution)/shard_map/ppermute | solution.py:26
  382.0 19.3 %collective-permute-done.13 = bf16[96,3352]{1,0:T(8,128)(2,1)S(1)} collective-permute-done((bf16[96,3352]{1,0:T(8,128)(2,1)S(1)}, bf16[96,3352]{1,0:T(8,128)(2,1)S(1)}, u32[]{:S(2)}, u32[]{:S(2)}) %collective-permute-start.13) | collective-permute-done | bytes 643616 | tf_op jit(solution)/shard_map/ppermute | solution.py:26
  405.5 9.5 collective-permute-done.15
  416.2 20.8 %all-reduce.28 = f32[192]{0:T(256)S(1)} all-reduce(f32[192]{0:T(256)S(1)} %multiply_dynamic-update-slice_fusion.1), channel_id=5, replica_groups=mesh['rep'=4,'shard'=8] {'shard'}, use_global_device_ids=true, to_apply=%add.28 | all-reduce | flops 192 | bytes 1536
  482.8 49.2 %all-reduce.32 = f32[192]{0:T(256)S(1)} all-reduce(f32[192]{0:T(256)S(1)} %multiply_dynamic-update-slice_fusion), channel_id=12, replica_groups=mesh['rep'=4,'shard'=8] {'shard'}, use_global_device_ids=true, to_apply=%add.32 | all-reduce | flops 192 | bytes 1536
  534.7 75.8 %all-gather.31.cloned.1.call-done = f32[192,128,64]{1,2,0:T(8,128)} async-done(((f32[24,128,64]{1,2,0:T(8,128)}), f32[192,128,64]{1,2,0:T(8,128)}) %all-gather.31.cloned.1.call-update) | async-done | bytes 6291472 | tf_op jit(solution)/shard_map/all_gather | solution.py:46
  622.6 40.6 %all-gather.33.cloned.1.call-done = bf16[1,1536,768]{2,1,0:T(8,128)(2,1)} async-done(((bf16[1,192,768]{2,1,0:T(8,128)(2,1)}), bf16[1,1536,768]{2,1,0:T(8,128)(2,1)}) %all-gather.33.cloned.1.call-update) | async-done | bytes 2359312 | tf_op jit(solution)/shard_map/all_gather | solution.py:146
  683.4 90.5 %all-gather.35.cloned.1.call-done = f32[192,128,64]{1,2,0:T(8,128)} async-done(((f32[24,128,64]{1,2,0:T(8,128)}), f32[192,128,64]{1,2,0:T(8,128)}) %all-gather.35.cloned.1.call-update) | async-done | bytes 6291472 | tf_op jit(solution)/shard_map/all_gather | solution.py:46
  775.2 50.7 %while.36 = (s32[]{:T(128)}, f32[24,128,64]{2,1,0:T(8,128)}, s32[]{:T(128)}, f32[8,24]{1,0:T(8,128)}, f32[8,24,128,64]{2,3,1,0:T(8,128)}, /*index=5*/s32[]{:T(128)}, s32[]{:T(128)}, s32[]{:T(128)}, s32[]{:T(128)}) while((s32[]{:T(128)}, f32[24,128,64]{2,1,0:T(8,128)}, s32[]{:T(128)}, f32[8,24]{1,0:T(8,128)}, f32[8,24,128,64]{2,3,1,0:T(8,128)}, ...), condition=%wide.region_15.17_spmd, body=%wide.region_14.16_spmd.sunk | while | flops 393222 | bytes 5505459 | solution.py:55
  895.8 6.7 fusion.169
  917.0 61.1 %all-gather.39.cloned.1.call-done = f32[192,128,64]{1,2,0:T(8,128)} async-done(((f32[24,128,64]{1,2,0:T(8,128)}), f32[192,128,64]{1,2,0:T(8,128)}) %all-gather.39.cloned.1.call-update) | async-done | bytes 6291472 | tf_op jit(solution)/shard_map/all_gather | solution.py:46
  979.4 50.2 %while.37 = (s32[]{:T(128)}, f32[24,128,64]{2,1,0:T(8,128)}, s32[]{:T(128)}, f32[8,24]{1,0:T(8,128)}, f32[8,24,128,64]{2,3,1,0:T(8,128)}, /*index=5*/s32[]{:T(128)}, s32[]{:T(128)}, s32[]{:T(128)}, s32[]{:T(128)}) while((s32[]{:T(128)}, f32[24,128,64]{2,1,0:T(8,128)}, s32[]{:T(128)}, f32[8,24]{1,0:T(8,128)}, f32[8,24,128,64]{2,3,1,0:T(8,128)}, ...), condition=%wide.region_30.32_spmd, body=%wide.region_29.31_spmd.sunk | while | flops 393222 | bytes 5505459 | solution.py:55
  1067.1 6.0 scatter-add.9
  1073.1 6.8 fusion.168
  1088.9 53.0 %reduce-scatter.17.cloned.1.call-done = f32[192,768]{1,0:T(8,128)} async-done(((f32[1536,768]{1,0:T(8,128)}), f32[192,768]{1,0:T(8,128)}) %reduce-scatter.17.cloned.1.call-update) | async-done | bytes 589840 | tf_op jit(solution)/shard_map/reduce_scatter | solution.py:252
  1141.9 98.8 %reduce-scatter.15.cloned.1.call-done = f32[192,768]{1,0:T(8,128)} async-done(((f32[1536,768]{1,0:T(8,128)}), f32[192,768]{1,0:T(8,128)}) %reduce-scatter.15.cloned.1.call-update) | async-done | bytes 589840 | tf_op jit(solution)/shard_map/reduce_scatter | solution.py:252
  1240.8 183.4 %reduce-scatter.13.cloned.1.call-done = f32[96,3352]{1,0:T(8,128)} async-done(((f32[768,3352]{1,0:T(8,128)}), f32[96,3352]{1,0:T(8,128)}) %reduce-scatter.13.cloned.1.call-update) | async-done | bytes 1287184 | tf_op jit(solution)/shard_map/reduce_scatter | solution.py:251
  1424.1 182.7 %reduce-scatter.11.cloned.1.call-done = f32[96,3352]{1,0:T(8,128)} async-done(((f32[768,3352]{1,0:T(8,128)}), f32[96,3352]{1,0:T(8,128)}) %reduce-scatter.11.cloned.1.call-update) | async-done | bytes 1287184 | tf_op jit(solution)/shard_map/reduce_scatter | solution.py:251
  1606.9 42.2 %psum.97 = f32[2,3,24]{2,1,0:T(4,128)S(1)} all-reduce(f32[2,3,24]{2,1,0:T(4,128)S(1)} %pad_maximum_fusion.11), channel_id=1, replica_groups=mesh['rep'=4,'shard'=8] {'rep','shard'}, use_global_device_ids=true, to_apply=%region_72.74 | all-reduce | flops 144 | bytes 1152 | tf_op jit(solution)/shard_map/psum | solution.py:267
  1649.7 46.2 %all-gather.41.cloned.1.call-done = bf16[1,768,3352]{2,1,0:T(8,128)(2,1)} async-done(((bf16[1,96,3352]{2,1,0:T(8,128)(2,1)}), bf16[1,768,3352]{2,1,0:T(8,128)(2,1)}) %all-gather.41.cloned.1.call-update) | async-done | bytes 5148688 | tf_op jit(solution)/shard_map/all_gather | solution.py:137
  1700.2 35.0 %all-reduce.40 = (f32[1792]{0:T(1024)S(1)}, f32[1792]{0:T(1024)S(1)}, f32[768]{0:T(1024)S(1)}, f32[768]{0:T(1024)S(1)}, f32[1536]{0:T(1024)S(1)}, /*index=5*/f32[1536]{0:T(1024)S(1)}) all-reduce(f32[1792]{0:T(1024)S(1)} %copy-done.114, f32[1792]{0:T(1024)S(1)} %copy-done.116, ...), channel_id=25, replica_groups=mesh['rep'=4,'shard'=8] {'shard'}, use_global_device_ids=true, to_apply=%region_62.64.clone | all-reduce | flops 8192 | bytes 65536
  1736.5 25.0 %reduce-scatter.19.cloned.1.call-done = f32[224,4]{1,0:T(8,128)} async-done(((f32[1792,4]{1,0:T(8,128)}), f32[224,4]{1,0:T(8,128)}) %reduce-scatter.19.cloned.1.call-update) | async-done | bytes 3600
  1762.4 10.8 all-reduce.41
  1775.6 67.1 %all-reduce.46.cloned.1.call-done = (f32[1,96,3352]{2,1,0:T(8,128)}, f32[1,96,3352]{2,1,0:T(8,128)}, f32[1,192,768]{2,1,0:T(8,128)}, f32[1,192,768]{2,1,0:T(8,128)}) async-done(((f32[1,96,3352]{2,1,0:T(8,128)}, f32[1,96,3352]{2,1,0:T(8,128)}, f32[1,192,768]{2,1,0:T(8,128)}, f32[1,192,768]{2,1,0:T(8,128)}), (f32[1,96,3352]{2,1,0:T(8,128)}, f32[1,96,3352]{2,1,0:T(8,128)}, f32[1,192,768]{2,1,0:T(8,128)}, ...) | async-done | bytes 3754000 | tf_op jit(solution)/shard_map/psum | solution.py:258
  (783 shorter events, 420.4 us)
Async XLA Ops:
  7.3 433.7 %all-gather.27.cloned.1.call-start = ((), (), s32[]{:S(2)}) async-start(), calls=%async_computation.10 | async-start | bytes 7077888 | tf_op jit(solution)/shard_map/all_gather | solution.py:46
  10.1 143.6 %collective-permute-start = (bf16[96,3352]{1,0:T(8,128)(2,1)S(1)}, bf16[96,3352]{1,0:T(8,128)(2,1)S(1)}, u32[]{:S(2)}, u32[]{:S(2)}) collective-permute-start(bf16[96,3352]{1,0:T(8,128)(2,1)S(1)} %get-tuple-element.950), channel_id=1, source_target_pairs={{0,1},{1,2},{2,3},{3,4},{4,5},{5,6},{6,7},{7,0},{8,9},{9,10},{10,1... | collective-permute-start | bytes 1930760 | tf_op jit(solution)/shard_map/ppermute | solution.py:26
  13.1 140.7 %collective-permute-start.1 = (bf16[96,3352]{1,0:T(8,128)(2,1)S(1)}, bf16[96,3352]{1,0:T(8,128)(2,1)S(1)}, u32[]{:S(2)}, u32[]{:S(2)}) collective-permute-start(bf16[96,3352]{1,0:T(8,128)(2,1)S(1)} %get-tuple-element.950), channel_id=1, source_target_pairs={{0,7},{1,0},{2,1},{3,2},{4,3},{5,4},{6,5},{7,6},{8,15},{9,8},{10,9... | collective-permute-start | bytes 1930760 | tf_op jit(solution)/shard_map/ppermute | solution.py:29
  16.2 134.8 %collective-permute-start.8 = (s32[3]{0:T(128)S(1)}, s32[3]{0:T(128)S(1)}, u32[]{:S(2)}, u32[]{:S(2)}) collective-permute-start(s32[3]{0:T(128)S(1)} %slice_bitcast_fusion.5), channel_id=1, source_target_pairs={{0,1},{1,2},{2,3},{3,4},{4,5},{5,6},{6,7},{8,9},{9,10},{10,11},{11... | collective-permute-start | bytes 44 | tf_op jit(solution)/shard_map/ppermute | solution.py:39
  153.7 27.8 %collective-permute-start.2 = (bf16[96,3352]{1,0:T(8,128)(2,1)S(1)}, bf16[96,3352]{1,0:T(8,128)(2,1)S(1)}, u32[]{:S(2)}, u32[]{:S(2)}) collective-permute-start(bf16[96,3352]{1,0:T(8,128)(2,1)S(1)} %collective-permute-done), channel_id=1, source_target_pairs={{0,1},{1,2},{2,3},{3,4},{4,5},{5,6},{6,7},{7,0},{8,9},{9,10},{10,1... | collective-permute-start | bytes 1930760 | tf_op jit(solution)/shard_map/ppermute | solution.py:26
  153.8 30.2 %collective-permute-start.3 = (bf16[96,3352]{1,0:T(8,128)(2,1)S(1)}, bf16[96,3352]{1,0:T(8,128)(2,1)S(1)}, u32[]{:S(2)}, u32[]{:S(2)}) collective-permute-start(bf16[96,3352]{1,0:T(8,128)(2,1)S(1)} %collective-permute-done.1), channel_id=1, source_target_pairs={{0,7},{1,0},{2,1},{3,2},{4,3},{5,4},{6,5},{7,6},{8,15},{9,8},{10,9... | collective-permute-start | bytes 1930760 | tf_op jit(solution)/shard_map/ppermute | solution.py:29
  181.5 24.2 %collective-permute-start.4 = (bf16[96,3352]{1,0:T(8,128)(2,1)S(1)}, bf16[96,3352]{1,0:T(8,128)(2,1)S(1)}, u32[]{:S(2)}, u32[]{:S(2)}) collective-permute-start(bf16[96,3352]{1,0:T(8,128)(2,1)S(1)} %collective-permute-done.2), channel_id=1, source_target_pairs={{0,1},{1,2},{2,3},{3,4},{4,5},{5,6},{6,7},{7,0},{8,9},{9,10},{10,1... | collective-permute-start | bytes 1930760 | tf_op jit(solution)/shard_map/ppermute | solution.py:26
  184.0 25.2 %collective-permute-start.5 = (bf16[96,3352]{1,0:T(8,128)(2,1)S(1)}, bf16[96,3352]{1,0:T(8,128)(2,1)S(1)}, u32[]{:S(2)}, u32[]{:S(2)}) collective-permute-start(bf16[96,3352]{1,0:T(8,128)(2,1)S(1)} %collective-permute-done.3), channel_id=1, source_target_pairs={{0,7},{1,0},{2,1},{3,2},{4,3},{5,4},{6,5},{7,6},{8,15},{9,8},{10,9... | collective-permute-start | bytes 1930760 | tf_op jit(solution)/shard_map/ppermute | solution.py:29
  205.8 13.4 collective-permute-start.6
  240.2 209.7 %all-gather.29.cloned.1.call-start = ((), (), s32[]{:S(2)}) async-start(), calls=%async_computation.11 | async-start | bytes 2654208 | tf_op jit(solution)/shard_map/all_gather | solution.py:146
  240.2 106.5 %collective-permute-start.9 = (bf16[96,3352]{1,0:T(8,128)(2,1)}, bf16[96,3352]{1,0:T(8,128)(2,1)}, u32[]{:S(2)}, u32[]{:S(2)}) collective-permute-start(bf16[96,3352]{1,0:T(8,128)(2,1)} %get-tuple-element.951), channel_id=1, source_target_pairs={{0,1},{1,2},{2,3},{3,4},{4,5},{5,6},{6,7},{7,0},{8,9},{9,10},{10,1... | collective-permute-start | bytes 1930760 | tf_op jit(solution)/shard_map/ppermute | solution.py:26
  242.6 106.2 %collective-permute-start.10 = (bf16[96,3352]{1,0:T(8,128)(2,1)}, bf16[96,3352]{1,0:T(8,128)(2,1)S(1)}, u32[]{:S(2)}, u32[]{:S(2)}) collective-permute-start(bf16[96,3352]{1,0:T(8,128)(2,1)} %get-tuple-element.951), channel_id=1, source_target_pairs={{0,7},{1,0},{2,1},{3,2},{4,3},{5,4},{6,5},{7,6},{8,15},{9,8},{10,9... | collective-permute-start | bytes 1930760 | tf_op jit(solution)/shard_map/ppermute | solution.py:29
  246.3 364.2 %all-gather.31.cloned.1.call-start = ((), (), s32[]{:S(2)}) async-start(), calls=%async_computation.12 | async-start | bytes 7077888 | tf_op jit(solution)/shard_map/all_gather | solution.py:46
  346.7 28.7 %collective-permute-start.11 = (bf16[96,3352]{1,0:T(8,128)(2,1)}, bf16[96,3352]{1,0:T(8,128)(2,1)S(1)}, u32[]{:S(2)}, u32[]{:S(2)}) collective-permute-start(bf16[96,3352]{1,0:T(8,128)(2,1)} %collective-permute-done.9), channel_id=1, source_target_pairs={{0,1},{1,2},{2,3},{3,4},{4,5},{5,6},{6,7},{7,0},{8,9},{9,10},{10,1... | collective-permute-start | bytes 1930760 | tf_op jit(solution)/shard_map/ppermute | solution.py:26
  348.8 29.8 %collective-permute-start.12 = (bf16[96,3352]{1,0:T(8,128)(2,1)S(1)}, bf16[96,3352]{1,0:T(8,128)(2,1)S(1)}, u32[]{:S(2)}, u32[]{:S(2)}) collective-permute-start(bf16[96,3352]{1,0:T(8,128)(2,1)S(1)} %collective-permute-done.10), channel_id=1, source_target_pairs={{0,7},{1,0},{2,1},{3,2},{4,3},{5,4},{6,5},{7,6},{8,15},{9,8},{10,9... | collective-permute-start | bytes 1930760 | tf_op jit(solution)/shard_map/ppermute | solution.py:29
  375.4 25.9 %collective-permute-start.13 = (bf16[96,3352]{1,0:T(8,128)(2,1)S(1)}, bf16[96,3352]{1,0:T(8,128)(2,1)S(1)}, u32[]{:S(2)}, u32[]{:S(2)}) collective-permute-start(bf16[96,3352]{1,0:T(8,128)(2,1)S(1)} %collective-permute-done.11), channel_id=1, source_target_pairs={{0,1},{1,2},{2,3},{3,4},{4,5},{5,6},{6,7},{7,0},{8,9},{9,10},{10,1... | collective-permute-start | bytes 1930760 | tf_op jit(solution)/shard_map/ppermute | solution.py:26
  378.6 26.0 %collective-permute-start.14 = (bf16[96,3352]{1,0:T(8,128)(2,1)S(1)}, bf16[96,3352]{1,0:T(8,128)(2,1)S(1)}, u32[]{:S(2)}, u32[]{:S(2)}) collective-permute-start(bf16[96,3352]{1,0:T(8,128)(2,1)S(1)} %collective-permute-done.12), channel_id=1, source_target_pairs={{0,7},{1,0},{2,1},{3,2},{4,3},{5,4},{6,5},{7,6},{8,15},{9,8},{10,9... | collective-permute-start | bytes 1930760 | tf_op jit(solution)/shard_map/ppermute | solution.py:29
  401.2 13.8 collective-permute-start.15
  481.9 181.3 %all-gather.33.cloned.1.call-start = ((), (), s32[]{:S(2)}) async-start(), calls=%async_computation.13 | async-start | bytes 2654208 | tf_op jit(solution)/shard_map/all_gather | solution.py:146
  482.4 291.4 %all-gather.35.cloned.1.call-start = ((), (), s32[]{:S(2)}) async-start(), calls=%async_computation.14 | async-start | bytes 7077888 | tf_op jit(solution)/shard_map/all_gather | solution.py:46
  671.4 195.7 %all-gather.37.cloned.1.call-start = ((), (), s32[]{:S(2)}) async-start(), calls=%async_computation.15 | async-start | bytes 5971968 | tf_op jit(solution)/shard_map/all_gather | solution.py:137
  672.0 306.1 %all-gather.39.cloned.1.call-start = ((), (), s32[]{:S(2)}) async-start(), calls=%async_computation.16 | async-start | bytes 7077888 | tf_op jit(solution)/shard_map/all_gather | solution.py:46
  847.4 11.3 collective-permute-start.17
  879.9 206.4 %reduce-scatter.21.cloned.1.call-start = ((), (), s32[]{:S(2)}) async-start(), calls=%async_computation.19 | async-start | bytes 1032192
  885.5 256.4 %reduce-scatter.17.cloned.1.call-start = ((), (), s32[]{:S(2)}) async-start(), calls=%async_computation.9 | async-start | bytes 5308416 | tf_op jit(solution)/shard_map/reduce_scatter | solution.py:252
  889.7 351.1 %reduce-scatter.15.cloned.1.call-start = ((), (), s32[]{:S(2)}) async-start(), calls=%async_computation.8 | async-start | bytes 5308416 | tf_op jit(solution)/shard_map/reduce_scatter | solution.py:252
  894.8 529.3 %reduce-scatter.13.cloned.1.call-start = ((), (), s32[]{:S(2)}) async-start(), calls=%async_computation.7 | async-start | bytes 11943936 | tf_op jit(solution)/shard_map/reduce_scatter | solution.py:251
  902.6 704.2 %reduce-scatter.11.cloned.1.call-start = ((), (), s32[]{:S(2)}) async-start(), calls=%async_computation.6 | async-start | bytes 11943936 | tf_op jit(solution)/shard_map/reduce_scatter | solution.py:251
  1052.3 10.6 collective-permute-start.18
  1079.9 615.9 %all-gather.41.cloned.1.call-start = ((), (), s32[]{:S(2)}) async-start(), calls=%async_computation.17 | async-start | bytes 5971968 | tf_op jit(solution)/shard_map/all_gather | solution.py:137
  1080.7 680.8 %reduce-scatter.19.cloned.1.call-start = ((), (), s32[]{:S(2)}) async-start(), calls=%async_computation.18 | async-start | bytes 1032192
  1088.8 753.9 %all-reduce.46.cloned.1.call-start = ((), (), s32[]{:S(2)}) async-start(), calls=%async_computation.20 | async-start | bytes 7667712 | tf_op jit(solution)/shard_map/psum | solution.py:258
  (212 other events, 3318.6 us)
Sparse Core Ops, SparseCore 0:
  240.3 122.7 all-gather.26
  365.9 69.4 all-gather.28
  482.0 128.5 all-gather.30
  613.2 49.9 all-gather.32
  671.5 102.2 all-gather.34
  775.9 85.5 all-gather.36
  880.0 98.0 all-gather.38
  981.4 62.0 reduce-scatter.20
  1047.2 94.6 reduce-scatter.16
  1145.4 95.2 reduce-scatter.14
  1244.4 179.7 reduce-scatter.12
  1427.6 179.1 reduce-scatter.10
  1609.0 86.8 all-gather.40
  1699.6 61.7 reduce-scatter.18
  1763.9 78.7 all-reduce.45
